TPU v7x, 32 devices: a whole 2x2x4 slice. The times are simulated.
32 devices in a mesh: dp: 8 (over y, x, core), ctx: 4 (over z).
Axes of the slice: x: 2, y: 2, z: 4, core: 2. Of those that a mesh axis runs over, the one named last changes fastest.
Arguments:
- frames: bfloat16 [8192, 1024], P(('dp', 'ctx')), parts along dimension 0, may hold values from -20 to 20
- tile_source: int32 [512], P('dp'), parts along dimension 0, may hold values from 0 to 63, as said below
- tile_utt: int32 [512], P('dp'), parts along dimension 0, may hold values from 0 to 3, never falling along the last dimension, each value on 1 to 33 neighbouring positions
- query_weight: bfloat16 [1024, 512], replicated, may hold values from -1.625 to 1.625
- key_weight: bfloat16 [1024, 512], replicated, may hold values from -0.1875 to 0.1875
- value_weight: bfloat16 [1024, 512], replicated, may hold values from -0.1875 to 0.1875
- output_weight: bfloat16 [512, 1024], replicated, may hold values from -1.5 to 1.5
- depth_weight: float32 [31, 1024], replicated, may hold values from -1 to 1
- bn_scale: float32 [1024], replicated, may hold values from 0.5 to 2
- bn_shift: float32 [1024], replicated, may hold values from -3 to 3
Outputs:
- encoded: bfloat16 [8192, 1024], P(('dp', 'ctx')), parts along dimension 0
There are 8 independent parts, one for each index of `dp`. A program takes and returns all parts, laid end to end along the dimension named above; an argument that names none is the same for every part. Nothing has to cross between parts.
Inputs may be any that keep to these rules, and one draw needn't show every extreme that they name: `tile_source`: A permutation of the tiles of a part. The tiles that one shard receives come at most 4 from any one shard, and exactly 4 from some shard; for one tile position within a shard, the sources over all shards lie on distinct shards. `tile_utt`: never falls along the tiles; each of the 4 utterances holds 1 to 33 tiles, one exactly 33.
All inputs are finite; a program needn't handle non-finite values.
Results may differ from a plain program's by a relative error of at most 0.0068.
Values may be sent and summed in bfloat16 or wider, within the bound.
No kernel may reach another device: no remote copies, remote signals or barrier semaphores. Data moves between devices by JAX's collectives and lax.ppermute only.
A program may use at most 64 MiB of HBM per device.

v0:
```python
import math
import jax
import jax.numpy as jnp
from jax import lax
from jax.sharding import PartitionSpec as P

HEADS = 4
HEAD_DIM = 128
KERNEL = 31
TILE = 16
NEGATIVE = -1e30


def extended_2(block, sides, width):
    for axis, dim in sides:
        count = lax.axis_size(axis)
        forward = [(i, i + 1) for i in range(count - 1)]
        backward = [(target, source) for source, target in forward]
        low = lax.ppermute(
            lax.slice_in_dim(block, block.shape[dim] - width, None, axis=dim), axis, forward
        )
        high = lax.ppermute(lax.slice_in_dim(block, 0, width, axis=dim), axis, backward)
        block = jnp.concatenate([low, block, high], axis=dim)
    return block


def layer_norm(rows):
    values = rows.astype(jnp.float32)
    center = values - jnp.mean(values, axis=-1, keepdims=True)
    spread = jnp.mean(center * center, axis=-1, keepdims=True)
    return center * lax.rsqrt(spread + 1e-05)


def local_utt(row_utt, first_row, rows_here, total_rows):
    positions = first_row + jnp.arange(rows_here, dtype=jnp.int32)
    inside = (positions >= 0) & (positions < total_rows)
    picked = jnp.take(row_utt, jnp.clip(positions, 0, total_rows - 1), axis=0)
    return jnp.where(inside, picked, -1)


def attend(carried, key_block, value_block, key_utt, queries, query_utt, score_scale):
    weighted, running_max, running_sum = carried
    scores = (
        jnp.einsum("qhd,khd->hqk", queries, key_block, preferred_element_type=jnp.float32)
        * score_scale
    )
    allowed = (query_utt[:, None] == key_utt[None, :])[None]
    block_max = jnp.max(jnp.where(allowed, scores, NEGATIVE), axis=-1, keepdims=True)
    new_max = jnp.maximum(running_max, block_max)
    factor = jnp.exp(running_max - new_max)
    weights = jnp.where(allowed, jnp.exp(scores - new_max), 0.0)
    running_sum = running_sum * factor + jnp.sum(weights, axis=-1, keepdims=True)
    weighted = weighted * factor + jnp.einsum(
        "hqk,khd->hqd",
        weights.astype(jnp.bfloat16),
        value_block,
        preferred_element_type=jnp.float32,
    )
    return (weighted, new_max, running_sum)


def pick_block(rows_here, rows_dev):
    shard_count = rows_here // rows_dev
    group_limit = max(1, 1024 // rows_dev)
    return rows_dev * max(
        [
            grouping
            for grouping in range(1, shard_count + 1)
            if shard_count % grouping == 0 and grouping <= group_limit
        ]
    )


def per_device(
    frames,
    tile_source,
    tile_utt,
    query_weight,
    key_weight,
    value_weight,
    output_weight,
    depth_weight,
    bn_scale,
    bn_shift,
):
    shard_count = lax.axis_size("ctx")
    my_index = lax.axis_index("ctx")
    rows_dev, feature_width = frames.shape
    tiles_dev = rows_dev // TILE
    tile_total = tiles_dev * shard_count
    total_rows = tile_total * TILE
    slot_count = (tiles_dev + shard_count - 1) // shard_count
    positions = jnp.arange(tile_total, dtype=jnp.int32)
    source_dev = tile_source // tiles_dev
    source_slot = tile_source % tiles_dev
    dest_dev = positions // tiles_dev
    earlier = (
        (dest_dev[:, None] == dest_dev[None, :])
        & (source_dev[:, None] == source_dev[None, :])
        & (positions[None, :] < positions[:, None])
    )
    arrival_rank = jnp.sum(earlier.astype(jnp.int32), axis=1)
    shards = jnp.arange(shard_count, dtype=jnp.int32)
    places = jnp.arange(slot_count, dtype=jnp.int32)
    matches = (
        (source_dev[None, None, :] == my_index)
        & (dest_dev[None, None, :] == shards[:, None, None])
        & (arrival_rank[None, None, :] == places[None, :, None])
    )
    chosen = jnp.sum(jnp.where(matches, source_slot[None, None, :], 0), axis=2).reshape(-1)
    filled = jnp.any(matches, axis=2).reshape(-1)
    tile_rows = frames.reshape(tiles_dev, TILE, feature_width)
    outgoing = jnp.where(
        filled[:, None, None], jnp.take(tile_rows, chosen, axis=0), jnp.zeros((), frames.dtype)
    )
    outgoing = outgoing.reshape(shard_count, slot_count, TILE, feature_width)
    arrived = lax.all_to_all(outgoing, "ctx", split_axis=0, concat_axis=0, tiled=True)
    mine_source = lax.dynamic_slice_in_dim(source_dev, my_index * tiles_dev, tiles_dev)
    mine_rank = lax.dynamic_slice_in_dim(arrival_rank, my_index * tiles_dev, tiles_dev)
    grouped = jnp.take(
        arrived.reshape(shard_count * slot_count, TILE, feature_width),
        mine_source * slot_count + mine_rank,
        axis=0,
    ).reshape(rows_dev, feature_width)
    normed = layer_norm(grouped).astype(jnp.bfloat16)
    queries = (
        jnp.dot(normed, query_weight, preferred_element_type=jnp.float32)
        .astype(jnp.bfloat16)
        .reshape(rows_dev, HEADS, HEAD_DIM)
    )
    key_rows = jnp.dot(normed, key_weight, preferred_element_type=jnp.float32).astype(jnp.bfloat16)
    value_rows = jnp.dot(normed, value_weight, preferred_element_type=jnp.float32).astype(
        jnp.bfloat16
    )
    key_value = jnp.stack([key_rows, value_rows])
    row_utt = jnp.repeat(tile_utt, TILE)
    query_utt = lax.dynamic_slice_in_dim(row_utt, my_index * rows_dev, rows_dev)
    score_scale = 1.0 / math.sqrt(HEAD_DIM)
    start_state = (
        jnp.zeros((HEADS, rows_dev, HEAD_DIM), jnp.float32),
        jnp.full((HEADS, rows_dev, 1), NEGATIVE, jnp.float32),
        jnp.zeros((HEADS, rows_dev, 1), jnp.float32),
    )

    def block_update(carried, block_pair, key_utt):
        rows_here = block_pair.shape[1]
        key_block = block_pair[0].reshape(rows_here, HEADS, HEAD_DIM)
        value_block = block_pair[1].reshape(rows_here, HEADS, HEAD_DIM)
        return attend(carried, key_block, value_block, key_utt, queries, query_utt, score_scale)

    fetched = lax.all_gather(key_value, "ctx", axis=1, tiled=True)
    rows_here = fetched.shape[1]
    block_rows = pick_block(rows_here, rows_dev)

    def one_block(block_index, inner):
        section = lax.dynamic_slice_in_dim(fetched, block_index * block_rows, block_rows, 1)
        key_utt = local_utt(row_utt, block_index * block_rows, block_rows, total_rows)
        return block_update(inner, section, key_utt)

    carried = lax.fori_loop(0, rows_here // block_rows, one_block, start_state)
    weighted, running_max, running_sum = carried
    attended = (
        jnp.transpose(weighted / running_sum, (1, 0, 2))
        .reshape(rows_dev, HEADS * HEAD_DIM)
        .astype(jnp.bfloat16)
    )
    residual = (
        grouped.astype(jnp.float32)
        + jnp.dot(attended, output_weight, preferred_element_type=jnp.float32)
    ).astype(jnp.bfloat16)
    shaped = layer_norm(residual).astype(jnp.bfloat16)
    margin = (KERNEL - 1) // 2
    extended = extended_2(shaped, (("ctx", 0),), margin).astype(jnp.float32)
    extended_utt = local_utt(
        row_utt, my_index * rows_dev - margin, rows_dev + 2 * margin, total_rows
    )
    convolved = jnp.zeros((rows_dev, feature_width), jnp.float32)
    for offset in range(KERNEL):
        aligned = (extended_utt[offset : offset + rows_dev] == query_utt)[:, None]
        convolved = (
            convolved
            + jnp.where(aligned, extended[offset : offset + rows_dev], 0.0) * depth_weight[offset]
        )
    activation = convolved * bn_scale + bn_shift
    return (residual.astype(jnp.float32) + activation * jax.nn.sigmoid(activation)).astype(
        jnp.bfloat16
    )


def solution(mesh):
    return jax.shard_map(
        per_device,
        mesh=mesh,
        in_specs=(P(("dp", "ctx"), None), P("dp"), P("dp"), P(), P(), P(), P(), P(), P(), P()),
        out_specs=P(("dp", "ctx"), None),
        check_vma=False,
    )
```

profile of v0, /device:TPU:0, one launch (start us, length us, event | category | flops | bytes accessed | tf_op | source)
XLA Modules:
  0.0 121.9 jit_solution(12822432287140586318)
XLA Ops:
  6.5 0.8 and_select_fusion.1
  7.4 0.7 broadcast_compare_fusion.1
  8.7 1.6 %gather_fusion.2 = bf16[16,16,1024]{2,1,0:T(8,128)(2,1)S(1)} fusion(bf16[16,16,1024]{2,1,0:T(8,128)(2,1)} %bitcast.80, s32[1024]{0:T(1024)S(1)} %pad_clamp_fusion.2), kind=kCustom, calls=%fused_computation.clone | custom fusion | bytes 1048640 | tf_op jit(solution)/shard_map/jit(_take)/gather | solution.py:114
  10.4 0.9 select_select_fusion
  11.3 6.3 %all-to-all-start = ((bf16[4,4,16,1024]{3,2,1,0:T(8,128)(2,1)}), bf16[4,4,16,1024]{3,2,1,0:T(8,128)(2,1)S(1)}, u32[]{:S(2)}, u32[]{:S(2)}) async-start(bf16[4,4,16,1024]{3,2,1,0:T(8,128)(2,1)} %bitcast.1), calls=%async_computation | async-start | bytes 1048576 | tf_op jit(solution)/shard_map/all_to_all | solution.py:117
  17.7 14.4 %all-to-all-done = bf16[4,4,16,1024]{3,2,1,0:T(8,128)(2,1)S(1)} async-done(((bf16[4,4,16,1024]{3,2,1,0:T(8,128)(2,1)}), bf16[4,4,16,1024]{3,2,1,0:T(8,128)(2,1)S(1)}, u32[]{:S(2)}, u32[]{:S(2)}) %all-to-all-start) | async-done | bytes 524320 | tf_op jit(solution)/shard_map/all_to_all | solution.py:117
  32.1 0.6 gather_fusion.3
  32.7 0.2 convert_reduce_fusion.1
  33.0 0.3 multiply_reduce_fusion
  33.7 0.4 fusion.18
  34.2 1.7 %fusion.19 = bf16[1,256,512]{2,1,0:T(8,128)(2,1)S(1)} fusion(bf16[256,1024]{1,0:T(8,128)(2,1)S(1)} %fusion.87, bf16[1024,512]{1,0:T(8,128)(2,1)} %param.17), kind=kOutput, calls=%fused_computation.27 | convolution fusion | flops 268566528 | bytes 1835008 | tf_op jit(solution)/shard_map/dot_general | solution.py:132
  35.9 0.8 pad_maximum_fusion
  36.9 1.7 %gather_fusion.1 = s32[286]{0:T(512)S(1)} fusion(s32[1024]{0:T(1024)S(1)} %reshape.320, s32[1024]{0:T(1024)S(1)} %pad_clamp_fusion), kind=kCustom, calls=%fused_computation.3 | custom fusion | bytes 3432 | tf_op jit(solution)/shard_map/jit(_take)/gather | solution.py:37
  38.6 4.5 %gather_fusion = s32[1024]{0:T(1024)S(1)} fusion(s32[1024]{0:T(1024)S(1)} %reshape.320, s32[1024]{0:T(1024)S(1)} %broadcast_clamp_fusion), kind=kCustom, calls=%fused_computation.2 | custom fusion | bytes 12288 | tf_op jit(solution)/shard_map/while/body/eval_jaxpr/jit(_take)/gather | solution.py:37
  43.2 0.6 slice_compare_fusion.30
  43.8 0.7 slice_compare_fusion.29
  44.9 1.2 fusion.17
  46.2 35.4 %all-gather.2.cloned.1.call-done = bf16[2,1024,512]{2,1,0:T(8,128)(2,1)} async-done(((bf16[2,256,512]{2,1,0:T(8,128)(2,1)}), bf16[2,1024,512]{2,1,0:T(8,128)(2,1)}) %all-gather.2.cloned.1.call-update) | async-done | bytes 2097168 | tf_op jit(solution)/shard_map/all_gather | solution.py:151
  81.7 3.0 %fusion.111 = (bf16[1,1024,512]{2,1,0:T(8,128)(2,1)}, bf16[1,1024,512]{2,1,0:T(8,128)(2,1)}) fusion(bf16[2,1024,512]{2,1,0:T(8,128)(2,1)} %all-gather.2.cloned.1.call-done), kind=kLoop, calls=%fused_computation.224 | loop fusion | bytes 4194304 | tf_op jit(solution)/shard_map/while/body/eval_jaxpr/slice | solution.py:147
  84.7 2.2 %squeeze.8 = bf16[1024,4,128]{2,1,0:T(4,128)(2,1)} reshape(bf16[1,1024,512]{2,1,0:T(8,128)(2,1)} %get-tuple-element.38) | data formatting | bytes 2097152 | tf_op jit(solution)/shard_map/while/body/eval_jaxpr/reshape;while/body/eval_jaxpr/squeeze | solution.py:147
  86.8 2.3 %select_reduce_fusion = (f32[4,256]{1,0:T(4,128)S(1)}, f32[4,256,1024]{2,1,0:T(8,128)S(1)}) fusion(pred[256,1024]{1,0:T(8,128)(4,1)S(1)} %broadcast_compare_fusion, bf16[1024,4,128]{2,1,0:T(4,128)(2,1)} %squeeze.8, bf16[32,4,8,128]{3,2,1,0:T(8,128)(2,1)S(1)} %copy-done.4), kind=kOutput, calls=%fused_computation.5 | convolution fusion | flops 271580160 | bytes 5771264 | tf_op jit(solution)/shard_map/while/body/eval_jaxpr/qhd,khd->hqk/dot_general | solution.py:44
  89.2 1.9 %copy-done.1 = f32[4,256,1024]{2,1,0:T(8,128)} copy-done((f32[4,256,1024]{2,1,0:T(8,128)}, f32[4,256,1024]{2,1,0:T(8,128)S(1)}, u32[]{:S(2)}) %copy-start.1) | copy-done | bytes 4194328
  91.1 1.4 %fusion = f32[4,256]{1,0:T(4,128)S(1)} fusion(f32[4,256,1024]{2,1,0:T(8,128)S(1)} %get-tuple-element.107, f32[4,256]{1,0:T(4,128)S(1)} %get-tuple-element.75, pred[256,1024]{1,0:T(8,128)(4,1)S(1)} %broadcast_compare_fusion), kind=kLoop, calls=%fused_computation.6 | loop fusion | flops 4193280 | bytes 4464640 | tf_op jit(solution)/shard_map/while/body/eval_jaxpr/reduce_sum | solution.py:52
  92.5 2.3 %copy.20 = bf16[1,1024,512]{1,2,0:T(8,128)(2,1)} copy(bf16[1,1024,512]{2,1,0:T(8,128)(2,1)} %get-tuple-element.40) | data formatting | bytes 2097152 | tf_op jit(solution)/shard_map/while/body/eval_jaxpr/reshape;while/body/eval_jaxpr/squeeze | solution.py:148
  94.8 3.6 %fusion.93 = bf16[256,4,128]{0,2,1:T(8,128)(2,1)S(1)} fusion(bf16[1024,4,128]{0,2,1:T(8,128)(2,1)} %bitcast.79, f32[4,256,1024]{2,1,0:T(8,128)} %copy-done.1, f32[4,256]{1,0:T(4,128)S(1)} %get-tuple-element.75, pred[256,1024]{1,0:T(8,128)(4,1)S(1)} %broadcast_compare_fusion, f32[256,4]{0,1:T(4,128)S(1)} %bitcast_add_fusion, f32[256,4]{0,1:T(4,128)S(1)} %get-tuple-element.74), kind=kOutput, calls=%fused_computation.132 | convolution fusion | flops 273022976 | bytes 5779456 | tf_op jit(solution)/shard_map/while/body/eval_jaxpr/hqk,khd->hqd/dot_general | solution.py:53
  98.6 0.5 convert_reduce_fusion
  99.2 0.3 fusion.20
  99.5 0.3 fusion.21
  99.8 2.1 %collective-permute-start = (bf16[15,1024]{1,0:T(8,128)(2,1)S(1)}, bf16[15,1024]{1,0:T(8,128)(2,1)S(1)}, u32[]{:S(2)}, u32[]{:S(2)}) collective-permute-start(bf16[15,1024]{1,0:T(8,128)(2,1)S(1)} %get-tuple-element.41), channel_id=1, source_target_pairs={{0,1},{1,2},{2,3},{4,5},{5,6},{6,7},{8,9},{9,10},{10,11},{12,13},{... | collective-permute-start | bytes 92168 | tf_op jit(solution)/shard_map/ppermute | solution.py:19
  101.9 1.3 %collective-permute-start.1 = (bf16[15,1024]{1,0:T(8,128)(2,1)S(1)}, bf16[15,1024]{1,0:T(8,128)(2,1)S(1)}, u32[]{:S(2)}, u32[]{:S(2)}) collective-permute-start(bf16[15,1024]{1,0:T(8,128)(2,1)S(1)} %get-tuple-element.42), channel_id=1, source_target_pairs={{1,0},{2,1},{3,2},{5,4},{6,5},{7,6},{9,8},{10,9},{11,10},{13,12},{... | collective-permute-start | bytes 92168 | tf_op jit(solution)/shard_map/ppermute | solution.py:22
  103.4 4.2 %collective-permute-done.1 = bf16[15,1024]{1,0:T(8,128)(2,1)S(1)} collective-permute-done((bf16[15,1024]{1,0:T(8,128)(2,1)S(1)}, bf16[15,1024]{1,0:T(8,128)(2,1)S(1)}, u32[]{:S(2)}, u32[]{:S(2)}) %collective-permute-start.1) | collective-permute-done | bytes 30752 | tf_op jit(solution)/shard_map/ppermute | solution.py:22
  108.0 7.0 %fusion.22 = bf16[256,1024]{1,0:T(8,128)(2,1)} fusion(bf16[256,1024]{1,0:T(8,128)(2,1)S(1)} %get-tuple-element.109, f32[286,1024]{1,0:T(8,128)S(1)} %maximum_convert_fusion, f32[1024]{0:T(1024)S(1)} %copy-done.6, f32[1024]{0:T(1024)S(1)} %copy-done.7, f32[1024]{0:T(1024)S(1)} %bitcast.92, f32[1024]{0:T(1024)S(1)} %bitcast.93, f32[1024]{0:T(1024)S(1)} %bitcast.95, ...), kind=kLoop, calls=%fused_computation.30 | loop fusion | flops 26476544 | bytes 33697536 | tf_op jit(solution)/shard_map/convert_element_type | solution.py:185
  (92 shorter events, 2.5 us)
Async XLA Ops:
  6.5 92.1 %copy-start = (bf16[512,1024]{1,0:T(8,128)(2,1)S(1)}, bf16[512,1024]{1,0:T(8,128)(2,1)}, u32[]{:S(2)}) copy-start(bf16[512,1024]{1,0:T(8,128)(2,1)} %param.18) | copy-start | bytes 3145732
  6.5 27.2 %copy-start.2 = (bf16[1024,512]{1,0:T(8,128)(2,1)S(1)}, bf16[1024,512]{1,0:T(8,128)(2,1)}, u32[]{:S(2)}) copy-start(bf16[1024,512]{1,0:T(8,128)(2,1)} %param.16) | copy-start | bytes 3145732
  11.3 20.8 %all-to-all-start = ((bf16[4,4,16,1024]{3,2,1,0:T(8,128)(2,1)}), bf16[4,4,16,1024]{3,2,1,0:T(8,128)(2,1)S(1)}, u32[]{:S(2)}, u32[]{:S(2)}) async-start(bf16[4,4,16,1024]{3,2,1,0:T(8,128)(2,1)} %bitcast.1), calls=%async_computation | async-start | bytes 1048576 | tf_op jit(solution)/shard_map/all_to_all | solution.py:117
  17.6 64.0 %all-gather.2.cloned.1.call-start = ((), (), s32[]{:S(2)}) async-start(), calls=%async_computation.1 | async-start | bytes 2621440 | tf_op jit(solution)/shard_map/all_gather | solution.py:151
  32.1 4.6 %copy-start.26 = (s32[64]{0:T(128)S(1)}, s32[64]{0:T(128)}, u32[]{:S(2)}) copy-start(s32[64]{0:T(128)} %param.14) | copy-start | bytes 772
  35.8 8.7 %copy-start.5 = (f32[31,1024]{1,0:T(8,128)S(1)}, f32[31,1024]{1,0:T(8,128)}, u32[]{:S(2)}) copy-start(f32[31,1024]{1,0:T(8,128)} %param.19) | copy-start | bytes 380932
  35.8 9.0 %copy-start.3 = (bf16[1024,512]{1,0:T(8,128)(2,1)S(1)}, bf16[1024,512]{1,0:T(8,128)(2,1)}, u32[]{:S(2)}) copy-start(bf16[1024,512]{1,0:T(8,128)(2,1)} %param.15) | copy-start | bytes 3145732
  46.1 40.8 %copy-start.4 = (bf16[32,4,8,128]{3,2,1,0:T(8,128)(2,1)S(1)}, bf16[32,4,8,128]{3,2,1,0:T(8,128)(2,1)}, u32[]{:S(2)}) copy-start(bf16[32,4,8,128]{3,2,1,0:T(8,128)(2,1)} %fusion.17) | copy-start | bytes 786436
  89.1 2.0 %copy-start.1 = (f32[4,256,1024]{2,1,0:T(8,128)}, f32[4,256,1024]{2,1,0:T(8,128)S(1)}, u32[]{:S(2)}) copy-start(f32[4,256,1024]{2,1,0:T(8,128)S(1)} %get-tuple-element.107) | copy-start | bytes 12582916
  98.4 9.4 %copy-start.6 = (f32[1024]{0:T(1024)S(1)}, f32[1024]{0:T(1024)}, u32[]{:S(2)}) copy-start(f32[1024]{0:T(1024)} %param.21) | copy-start | bytes 12292
  98.4 9.4 %copy-start.7 = (f32[1024]{0:T(1024)S(1)}, f32[1024]{0:T(1024)}, u32[]{:S(2)}) copy-start(f32[1024]{0:T(1024)} %param.20) | copy-start | bytes 12292
  98.4 9.4 %copy-start.8 = (pred[256]{0:T(512)(128)(4,1)S(1)}, pred[256]{0:T(512)(128)(4,1)}, u32[]{:S(2)}) copy-start(pred[256]{0:T(512)(128)(4,1)} %get-tuple-element.77) | copy-start | bytes 772
  98.4 9.4 %copy-start.9 = (pred[256]{0:T(512)(128)(4,1)S(1)}, pred[256]{0:T(512)(128)(4,1)}, u32[]{:S(2)}) copy-start(pred[256]{0:T(512)(128)(4,1)} %get-tuple-element.78) | copy-start | bytes 772
  98.4 9.4 %copy-start.10 = (pred[256]{0:T(512)(128)(4,1)S(1)}, pred[256]{0:T(512)(128)(4,1)}, u32[]{:S(2)}) copy-start(pred[256]{0:T(512)(128)(4,1)} %get-tuple-element.79) | copy-start | bytes 772
  98.5 9.4 %copy-start.11 = (pred[256]{0:T(512)(128)(4,1)S(1)}, pred[256]{0:T(512)(128)(4,1)}, u32[]{:S(2)}) copy-start(pred[256]{0:T(512)(128)(4,1)} %get-tuple-element.80) | copy-start | bytes 772
  98.5 9.4 %copy-start.12 = (pred[256]{0:T(512)(128)(4,1)S(1)}, pred[256]{0:T(512)(128)(4,1)}, u32[]{:S(2)}) copy-start(pred[256]{0:T(512)(128)(4,1)} %get-tuple-element.81) | copy-start | bytes 772
  98.5 9.4 %copy-start.13 = (pred[256]{0:T(512)(128)(4,1)S(1)}, pred[256]{0:T(512)(128)(4,1)}, u32[]{:S(2)}) copy-start(pred[256]{0:T(512)(128)(4,1)} %get-tuple-element.82) | copy-start | bytes 772
  98.5 9.4 %copy-start.14 = (pred[256]{0:T(512)(128)(4,1)S(1)}, pred[256]{0:T(512)(128)(4,1)}, u32[]{:S(2)}) copy-start(pred[256]{0:T(512)(128)(4,1)} %get-tuple-element.83) | copy-start | bytes 772
  98.5 9.4 %copy-start.15 = (pred[256]{0:T(512)(128)(4,1)S(1)}, pred[256]{0:T(512)(128)(4,1)}, u32[]{:S(2)}) copy-start(pred[256]{0:T(512)(128)(4,1)} %get-tuple-element.84) | copy-start | bytes 772
  98.5 9.4 %copy-start.16 = (pred[256]{0:T(512)(128)(4,1)S(1)}, pred[256]{0:T(512)(128)(4,1)}, u32[]{:S(2)}) copy-start(pred[256]{0:T(512)(128)(4,1)} %get-tuple-element.85) | copy-start | bytes 772
  98.5 9.4 %copy-start.17 = (pred[256]{0:T(512)(128)(4,1)S(1)}, pred[256]{0:T(512)(128)(4,1)}, u32[]{:S(2)}) copy-start(pred[256]{0:T(512)(128)(4,1)} %get-tuple-element.86) | copy-start | bytes 772
  98.5 9.4 %copy-start.18 = (pred[256]{0:T(512)(128)(4,1)S(1)}, pred[256]{0:T(512)(128)(4,1)}, u32[]{:S(2)}) copy-start(pred[256]{0:T(512)(128)(4,1)} %get-tuple-element.87) | copy-start | bytes 772
  98.5 9.4 %copy-start.19 = (pred[256]{0:T(512)(128)(4,1)S(1)}, pred[256]{0:T(512)(128)(4,1)}, u32[]{:S(2)}) copy-start(pred[256]{0:T(512)(128)(4,1)} %get-tuple-element.88) | copy-start | bytes 772
  98.5 9.4 %copy-start.20 = (pred[256]{0:T(512)(128)(4,1)S(1)}, pred[256]{0:T(512)(128)(4,1)}, u32[]{:S(2)}) copy-start(pred[256]{0:T(512)(128)(4,1)} %get-tuple-element.89) | copy-start | bytes 772
  98.6 9.4 %copy-start.21 = (pred[256]{0:T(512)(128)(4,1)S(1)}, pred[256]{0:T(512)(128)(4,1)}, u32[]{:S(2)}) copy-start(pred[256]{0:T(512)(128)(4,1)} %get-tuple-element.90) | copy-start | bytes 772
  98.6 9.4 %copy-start.22 = (pred[256]{0:T(512)(128)(4,1)S(1)}, pred[256]{0:T(512)(128)(4,1)}, u32[]{:S(2)}) copy-start(pred[256]{0:T(512)(128)(4,1)} %get-tuple-element.91) | copy-start | bytes 772
  98.6 9.4 %copy-start.23 = (pred[256]{0:T(512)(128)(4,1)S(1)}, pred[256]{0:T(512)(128)(4,1)}, u32[]{:S(2)}) copy-start(pred[256]{0:T(512)(128)(4,1)} %get-tuple-element.92) | copy-start | bytes 772
  98.6 9.4 %copy-start.24 = (pred[256]{0:T(512)(128)(4,1)S(1)}, pred[256]{0:T(512)(128)(4,1)}, u32[]{:S(2)}) copy-start(pred[256]{0:T(512)(128)(4,1)} %get-tuple-element.93) | copy-start | bytes 772
  98.6 9.4 %copy-start.25 = (pred[256]{0:T(512)(128)(4,1)S(1)}, pred[256]{0:T(512)(128)(4,1)}, u32[]{:S(2)}) copy-start(pred[256]{0:T(512)(128)(4,1)} %get-tuple-element.22) | copy-start | bytes 772
  99.8 3.7 %collective-permute-start = (bf16[15,1024]{1,0:T(8,128)(2,1)S(1)}, bf16[15,1024]{1,0:T(8,128)(2,1)S(1)}, u32[]{:S(2)}, u32[]{:S(2)}) collective-permute-start(bf16[15,1024]{1,0:T(8,128)(2,1)S(1)} %get-tuple-element.41), channel_id=1, source_target_pairs={{0,1},{1,2},{2,3},{4,5},{5,6},{6,7},{8,9},{9,10},{10,11},{12,13},{... | collective-permute-start | bytes 92168 | tf_op jit(solution)/shard_map/ppermute | solution.py:19
  101.9 5.8 %collective-permute-start.1 = (bf16[15,1024]{1,0:T(8,128)(2,1)S(1)}, bf16[15,1024]{1,0:T(8,128)(2,1)S(1)}, u32[]{:S(2)}, u32[]{:S(2)}) collective-permute-start(bf16[15,1024]{1,0:T(8,128)(2,1)S(1)} %get-tuple-element.42), channel_id=1, source_target_pairs={{1,0},{2,1},{3,2},{5,4},{6,5},{7,6},{9,8},{10,9},{11,10},{13,12},{... | collective-permute-start | bytes 92168 | tf_op jit(solution)/shard_map/ppermute | solution.py:22
Sparse Core Ops, SparseCore 0:
  36.8 44.7 all-gather.1
where the time goes:
time: 122 us
  waiting for transfers between devices  54.3 us (45%)
  local copies, waits for them, and re-layouts  18.6 us (15%)
  other arithmetic  15.6 us (13%)
  between operations  14 us (11%)
  starting transfers between devices  9.73 us (8%)
  matrix products  9.73 us (8%)
    all_gather x1, waiting for transfers between devices, per_device(): fetched = lax.all_gather(key_value, 'ctx', axis=1, tiled=True)  35.4 us
    all_to_all x1, waiting for transfers between devices, per_device(): lax.all_to_all(outgoing, 'ctx', split_axis=0, concat_axis=0, tiled=True)  14.4 us
    convert_element_type x1, other arithmetic, per_device(): (residual.astype(jnp.float32) + activation * jax.nn.sigmoid(activation))....  7.03 us
    all_to_all x1, starting transfers between devices, per_device(): lax.all_to_all(outgoing, 'ctx', split_axis=0, concat_axis=0, tiled=True)  6.35 us
    gather x2, local copies, waits for them, and re-layouts, local_utt(): picked = jnp.take(row_utt, jnp.clip(positions, 0, total_rows - 1), axis=0)  6.22 us
    ppermute x1, waiting for transfers between devices, extended_2(): lax.ppermute(lax.slice_in_dim(block, 0, width, axis=dim), axis, backward)  4.23 us
    dot_general x1, matrix products, attend(): jnp.einsum('hqk,khd->hqd', weights.astype(jnp.bfloat16), value_block, pre...  3.63 us
    slice x1, local copies, waits for them, and re-layouts, block_update(): key_block = block_pair[0].reshape(rows_here, HEADS, HEAD_DIM)  3.01 us
  transfers between devices with their start and end apart: 4, of which 4 were waited for; matrix products, arithmetic and copies ran while one was open for 8% of the time, Pallas kernels for 0%

commit v1 on v0

--- a/solution.py
+++ b/solution.py
@@ -148,7 +148,12 @@
         value_block = block_pair[1].reshape(rows_here, HEADS, HEAD_DIM)
         return attend(carried, key_block, value_block, key_utt, queries, query_utt, score_scale)
 
-    fetched = lax.all_gather(key_value, "ctx", axis=1, tiled=True)
+    ring = [key_value]
+    for hop in range(3):
+        ring.append(lax.ppermute(ring[-1], "ctx", [(dev, (dev + 1) % 4) for dev in range(4)]))
+    fetched = jnp.roll(
+        jnp.concatenate(ring[::-1], axis=1), (lax.axis_index("ctx") + 1) * ring[0].shape[1], axis=1
+    )
     rows_here = fetched.shape[1]
     block_rows = pick_block(rows_here, rows_dev)
 

time: 122 us -> 106 us (0.87)
  between operations: 14 us -> 0.94 us
  waiting for transfers between devices: 54.3 us -> 46.8 us
  other arithmetic: 15.6 us -> 18.3 us
    all_gather x1 -> x0, waiting for transfers between devices: 35.4 us -> none  [per_device(): fetched = lax.all_gather(key_value, 'ctx', axis=1, tiled=True)]
    ppermute x0 -> x3, waiting for transfers between devices: none -> 30.6 us  [per_device(): lax.ppermute(ring[-1], 'ctx', [(dev, (dev + 1) % 4) for dev in range(4)])]
    unnamed x54 -> x96, local copies, waits for them, and re-layouts: 2.06 us -> 6.51 us
    slice x1, local copies, waits for them, and re-layouts: 3.01 us -> 0.17 us  [block_update(): key_block = block_pair[0].reshape(rows_here, HEADS, HEAD_DIM)]
    all_to_all x1, waiting for transfers between devices: 14.4 us -> 11.8 us  [per_device(): lax.all_to_all(outgoing, 'ctx', split_axis=0, concat_axis=0, tiled=True)]
    squeeze x1, local copies, waits for them, and re-layouts: 2.29 us -> 0.54 us  [block_update(): value_block = block_pair[1].reshape(rows_here, HEADS, HEAD_DIM)]
    convert_element_type x1, other arithmetic: 0.14 us -> 1.85 us  [per_device(): grouped.astype(jnp.float32)]
    slice x2, local copies, waits for them, and re-layouts: 0.1 us -> 1.34 us  [per_device(): depth_weight[offset]]
  transfers between devices with their start and end apart: 4 -> 6, of which waited for: 4 -> 6; matrix products, arithmetic and copies ran while one was open for 8% -> 14% of each run, Pallas kernels for 0% -> 0%
where the time goes in v1:
time: 106 us; the launch traced here: 105 us
  waiting for transfers between devices  46.8 us (44%)
  local copies, waits for them, and re-layouts  19.3 us (18%)
  other arithmetic  18.3 us (17%)
  matrix products  10.8 us (10%)
  starting transfers between devices  8.94 us (8%)
    ppermute x3, waiting for transfers between devices, per_device(): lax.ppermute(ring[-1], 'ctx', [(dev, (dev + 1) % 4) for dev in range(4)])  30.6 us
    all_to_all x1, waiting for transfers between devices, per_device(): lax.all_to_all(outgoing, 'ctx', split_axis=0, concat_axis=0, tiled=True)  11.8 us
    convert_element_type x1, other arithmetic, per_device(): (residual.astype(jnp.float32) + activation * jax.nn.sigmoid(activation))....  7.95 us
    unnamed x96, local copies, waits for them, and re-layouts  6.51 us
    all_to_all x1, starting transfers between devices, per_device(): lax.all_to_all(outgoing, 'ctx', split_axis=0, concat_axis=0, tiled=True)  6.35 us
    gather x2, local copies, waits for them, and re-layouts, local_utt(): picked = jnp.take(row_utt, jnp.clip(positions, 0, total_rows - 1), axis=0)  6.22 us
    ppermute x1, waiting for transfers between devices, extended_2(): lax.ppermute(lax.slice_in_dim(block, 0, width, axis=dim), axis, backward)  4.23 us
    dot_general x1, matrix products, attend(): jnp.einsum('hqk,khd->hqd', weights.astype(jnp.bfloat16), value_block, pre...  3.41 us
  transfers between devices with their start and end apart: 6, of which 6 were waited for; matrix products, arithmetic and copies ran while one was open for 14% of the time, Pallas kernels for 0%

profile of v1, /device:TPU:0, one launch (start us, length us, event | category | flops | bytes accessed | tf_op | source)
XLA Modules:
  0.0 105.1 jit_solution(6335966125199071597)
XLA Ops:
  0.0 0.8 and_select_fusion.1
  0.8 0.7 broadcast_compare_fusion.1
  2.1 1.7 %gather_fusion.2 = bf16[16,16,1024]{2,1,0:T(8,128)(2,1)S(1)} fusion(bf16[16,16,1024]{2,1,0:T(8,128)(2,1)} %bitcast.80, s32[1024]{0:T(1024)S(1)} %pad_clamp_fusion.2), kind=kCustom, calls=%fused_computation.clone | custom fusion | bytes 1048640 | tf_op jit(solution)/shard_map/jit(_take)/gather | solution.py:114
  3.9 0.9 select_select_fusion
  4.8 6.3 %all-to-all-start = ((bf16[4,4,16,1024]{3,2,1,0:T(8,128)(2,1)}), bf16[4,4,16,1024]{3,2,1,0:T(8,128)(2,1)S(1)}, u32[]{:S(2)}, u32[]{:S(2)}) async-start(bf16[4,4,16,1024]{3,2,1,0:T(8,128)(2,1)} %bitcast.1), calls=%async_computation | async-start | bytes 1048576 | tf_op jit(solution)/shard_map/all_to_all | solution.py:117
  11.1 0.7 broadcast_in_dim.349
  12.0 1.7 %gather_fusion.1 = s32[286]{0:T(512)S(1)} fusion(s32[1024]{0:T(1024)S(1)} %reshape.320, s32[1024]{0:T(1024)S(1)} %get-tuple-element.112), kind=kCustom, calls=%fused_computation.3 | custom fusion | bytes 3432 | tf_op jit(solution)/shard_map/jit(_take)/gather | solution.py:37
  13.8 11.8 %all-to-all-done = bf16[4,4,16,1024]{3,2,1,0:T(8,128)(2,1)S(1)} async-done(((bf16[4,4,16,1024]{3,2,1,0:T(8,128)(2,1)}), bf16[4,4,16,1024]{3,2,1,0:T(8,128)(2,1)S(1)}, u32[]{:S(2)}, u32[]{:S(2)}) %all-to-all-start) | async-done | bytes 524320 | tf_op jit(solution)/shard_map/all_to_all | solution.py:117
  27.7 1.7 %fusion.19 = bf16[1,256,512]{2,1,0:T(8,128)(2,1)S(1)} fusion(bf16[256,1024]{1,0:T(8,128)(2,1)S(1)} %fusion.87, bf16[1024,512]{1,0:T(8,128)(2,1)} %param.17), kind=kOutput, calls=%fused_computation.27 | convolution fusion | flops 268566528 | bytes 1835008 | tf_op jit(solution)/shard_map/dot_general | solution.py:132
  29.4 0.8 pad_maximum_fusion
  30.2 4.5 %gather_fusion = s32[1024]{0:T(1024)S(1)} fusion(s32[1024]{0:T(1024)S(1)} %reshape.320, s32[1024]{0:T(1024)S(1)} %get-tuple-element.113), kind=kCustom, calls=%fused_computation.2 | custom fusion | bytes 12288 | tf_op jit(solution)/shard_map/while/body/eval_jaxpr/jit(_take)/gather | solution.py:37
  34.8 0.6 fusion.113
  35.4 9.7 %collective-permute-done = bf16[2,256,512]{2,1,0:T(8,128)(2,1)S(1)} collective-permute-done((bf16[2,256,512]{2,1,0:T(8,128)(2,1)}, bf16[2,256,512]{2,1,0:T(8,128)(2,1)S(1)}, u32[]{:S(2)}, u32[]{:S(2)}) %collective-permute-start) | collective-permute-done | bytes 524320 | tf_op jit(solution)/shard_map/ppermute | solution.py:153
  45.8 0.7 fusion.112
  46.7 12.4 %collective-permute-done.1 = bf16[2,256,512]{2,1,0:T(8,128)(2,1)} collective-permute-done((bf16[2,256,512]{2,1,0:T(8,128)(2,1)S(1)}, bf16[2,256,512]{2,1,0:T(8,128)(2,1)}, u32[]{:S(2)}, u32[]{:S(2)}) %collective-permute-start.1) | collective-permute-done | bytes 524320 | tf_op jit(solution)/shard_map/ppermute | solution.py:153
  59.1 0.7 slice_compare_fusion.29
  59.9 2.4 %fusion.17 = bf16[32,4,8,128]{3,2,1,0:T(8,128)(2,1)} fusion(bf16[256,1024]{1,0:T(8,128)(2,1)S(1)} %fusion.87, bf16[1024,512]{1,0:T(8,128)(2,1)} %param.15), kind=kOutput, calls=%fused_computation.25 | convolution fusion | flops 268566528 | bytes 1835008 | tf_op jit(solution)/shard_map/dot_general | solution.py:127
  62.2 1.9 %fusion.110 = f32[16,16,1024]{2,1,0:T(8,128)} fusion(bf16[16,16,1024]{2,1,0:T(8,128)(2,1)S(1)} %gather_fusion.3, pred[16]{0:T(512)(128)(4,1)} %copy-done.36), kind=kLoop, calls=%fused_computation.233 | loop fusion | flops 524288 | bytes 1572880 | tf_op jit(solution)/shard_map/convert_element_type | solution.py:173
  64.1 8.4 %collective-permute-done.2 = bf16[2,256,512]{2,1,0:T(8,128)(2,1)} collective-permute-done((bf16[2,256,512]{2,1,0:T(8,128)(2,1)}, bf16[2,256,512]{2,1,0:T(8,128)(2,1)}, u32[]{:S(2)}, u32[]{:S(2)}) %collective-permute-start.2) | collective-permute-done | bytes 524320 | tf_op jit(solution)/shard_map/ppermute | solution.py:153
  72.5 1.1 %constant_dynamic-update-slice_fusion.7 = bf16[2,2048,512]{2,1,0:T(8,128)(2,1)S(1)} fusion(bf16[2,256,512]{2,1,0:T(8,128)(2,1)} %collective-permute-done.2), kind=kLoop, calls=%fused_computation.152 | loop fusion | bytes 1048576
  73.5 1.1 %constant_dynamic-update-slice_fusion.6 = bf16[2,2048,512]{2,1,0:T(8,128)(2,1)S(1)} fusion(bf16[2,2048,512]{2,1,0:T(8,128)(2,1)S(1)} %constant_dynamic-update-slice_fusion.7, bf16[2,256,512]{2,1,0:T(8,128)(2,1)} %collective-permute-done.1), kind=kLoop, calls=%fused_computation.151 | loop fusion | bytes 1048576
  74.7 1.1 %constant_dynamic-update-slice_fusion.3 = bf16[2,2048,512]{2,1,0:T(8,128)(2,1)S(1)} fusion(bf16[2,2048,512]{2,1,0:T(8,128)(2,1)S(1)} %constant_dynamic-update-slice_fusion.4, bf16[2,256,512]{2,1,0:T(8,128)(2,1)} %collective-permute-done.2), kind=kLoop, calls=%fused_computation.148 | loop fusion | bytes 1048576
  75.8 1.1 %constant_dynamic-update-slice_fusion.2 = bf16[2,2048,512]{2,1,0:T(8,128)(2,1)S(1)} fusion(bf16[2,2048,512]{2,1,0:T(8,128)(2,1)S(1)} %constant_dynamic-update-slice_fusion.3, bf16[2,256,512]{2,1,0:T(8,128)(2,1)} %collective-permute-done.1), kind=kLoop, calls=%fused_computation.147 | loop fusion | bytes 1048576
  77.1 1.1 %squeeze.8 = bf16[1024,4,128]{2,1,0:T(4,128)(2,1)} reshape(bf16[1,1024,512]{2,1,0:T(8,128)(2,1)S(1)} %get-tuple-element.38) | data formatting | bytes 2097152 | tf_op jit(solution)/shard_map/while/body/eval_jaxpr/reshape;while/body/eval_jaxpr/squeeze | solution.py:147
  78.3 2.4 %select_reduce_fusion = (f32[4,256]{1,0:T(4,128)S(1)}, f32[4,256,1024]{2,1,0:T(8,128)S(1)}) fusion(pred[256,1024]{1,0:T(8,128)(4,1)S(1)} %broadcast_compare_fusion, bf16[1024,4,128]{2,1,0:T(4,128)(2,1)} %squeeze.8, bf16[32,4,8,128]{3,2,1,0:T(8,128)(2,1)} %fusion.17), kind=kOutput, calls=%fused_computation.5 | convolution fusion | flops 271580160 | bytes 5771264 | tf_op jit(solution)/shard_map/while/body/eval_jaxpr/qhd,khd->hqk/dot_general | solution.py:44
  80.7 1.9 %copy-done.1 = f32[4,256,1024]{2,1,0:T(8,128)} copy-done((f32[4,256,1024]{2,1,0:T(8,128)}, f32[4,256,1024]{2,1,0:T(8,128)S(1)}, u32[]{:S(2)}) %copy-start.1) | copy-done | bytes 4194328
  82.6 1.4 %fusion = f32[4,256]{1,0:T(4,128)S(1)} fusion(f32[4,256,1024]{2,1,0:T(8,128)S(1)} %get-tuple-element.107, f32[4,256]{1,0:T(4,128)S(1)} %get-tuple-element.75, pred[256,1024]{1,0:T(8,128)(4,1)S(1)} %broadcast_compare_fusion), kind=kLoop, calls=%fused_computation.6 | loop fusion | flops 4193280 | bytes 4464640 | tf_op jit(solution)/shard_map/while/body/eval_jaxpr/reduce_sum | solution.py:52
  84.5 3.4 %fusion.93 = bf16[256,4,128]{0,2,1:T(8,128)(2,1)S(1)} fusion(bf16[1024,4,128]{0,2,1:T(8,128)(2,1)S(1)} %bitcast.79, f32[4,256,1024]{2,1,0:T(8,128)} %copy-done.1, f32[4,256]{1,0:T(4,128)S(1)} %get-tuple-element.75, pred[256,1024]{1,0:T(8,128)(4,1)S(1)} %broadcast_compare_fusion, f32[256,4]{0,1:T(4,128)S(1)} %bitcast_add_fusion, ...), kind=kOutput, calls=%fused_computation.132 | convolution fusion | flops 273022976 | bytes 5779456 | tf_op jit(solution)/shard_map/while/body/eval_jaxpr/hqk,khd->hqd/dot_general | solution.py:53
  89.5 1.3 %collective-permute-start.3 = (bf16[15,1024]{1,0:T(8,128)(2,1)S(1)}, bf16[15,1024]{1,0:T(8,128)(2,1)S(1)}, u32[]{:S(2)}, u32[]{:S(2)}) collective-permute-start(bf16[15,1024]{1,0:T(8,128)(2,1)S(1)} %get-tuple-element.41), channel_id=1, source_target_pairs={{0,1},{1,2},{2,3},{4,5},{5,6},{6,7},{8,9},{9,10},{10,11},{12,13},{... | collective-permute-start | bytes 92168 | tf_op jit(solution)/shard_map/ppermute | solution.py:19
  90.8 1.3 %collective-permute-start.4 = (bf16[15,1024]{1,0:T(8,128)(2,1)S(1)}, bf16[15,1024]{1,0:T(8,128)(2,1)S(1)}, u32[]{:S(2)}, u32[]{:S(2)}) collective-permute-start(bf16[15,1024]{1,0:T(8,128)(2,1)S(1)} %get-tuple-element.42), channel_id=1, source_target_pairs={{1,0},{2,1},{3,2},{5,4},{6,5},{7,6},{9,8},{10,9},{11,10},{13,12},{... | collective-permute-start | bytes 92168 | tf_op jit(solution)/shard_map/ppermute | solution.py:22
  92.4 4.2 %collective-permute-done.4 = bf16[15,1024]{1,0:T(8,128)(2,1)S(1)} collective-permute-done((bf16[15,1024]{1,0:T(8,128)(2,1)S(1)}, bf16[15,1024]{1,0:T(8,128)(2,1)S(1)}, u32[]{:S(2)}, u32[]{:S(2)}) %collective-permute-start.4) | collective-permute-done | bytes 30752 | tf_op jit(solution)/shard_map/ppermute | solution.py:22
  97.1 8.0 %fusion.22 = bf16[256,1024]{1,0:T(8,128)(2,1)} fusion(bf16[256,1024]{1,0:T(8,128)(2,1)S(1)} %get-tuple-element.109, f32[286,1024]{1,0:T(8,128)S(1)} %maximum_convert_fusion, f32[1024]{0:T(1024)S(1)} %copy-done.37, f32[1024]{0:T(1024)S(1)} %copy-done.38, f32[1024]{0:T(1024)S(1)} %bitcast.92, f32[1024]{0:T(1024)S(1)} %bitcast.93, f32[1024]{0:T(1024)S(1)} %bitcast.95, ...), kind=kLoop, calls=%fused_computation.30 | loop fusion | flops 26476544 | bytes 33697536 | tf_op jit(solution)/shard_map/convert_element_type | solution.py:190
  (138 shorter events, 6.3 us)
Async XLA Ops:
  0.0 88.3 %copy-start = (bf16[512,1024]{1,0:T(8,128)(2,1)S(1)}, bf16[512,1024]{1,0:T(8,128)(2,1)}, u32[]{:S(2)}) copy-start(bf16[512,1024]{1,0:T(8,128)(2,1)} %param.18) | copy-start | bytes 3145732
  2.1 25.1 %copy-start.3 = (bf16[1024,512]{1,0:T(8,128)(2,1)S(1)}, bf16[1024,512]{1,0:T(8,128)(2,1)}, u32[]{:S(2)}) copy-start(bf16[1024,512]{1,0:T(8,128)(2,1)} %param.16) | copy-start | bytes 3145732
  4.8 20.8 %all-to-all-start = ((bf16[4,4,16,1024]{3,2,1,0:T(8,128)(2,1)}), bf16[4,4,16,1024]{3,2,1,0:T(8,128)(2,1)S(1)}, u32[]{:S(2)}, u32[]{:S(2)}) async-start(bf16[4,4,16,1024]{3,2,1,0:T(8,128)(2,1)} %bitcast.1), calls=%async_computation | async-start | bytes 1048576 | tf_op jit(solution)/shard_map/all_to_all | solution.py:117
  13.8 16.4 %copy-start.36 = (pred[16]{0:T(512)(128)(4,1)}, pred[16]{0:T(512)(128)(4,1)S(1)}, u32[]{:S(2)}) copy-start(pred[16]{0:T(512)(128)(4,1)S(1)} %get-tuple-element.24) | copy-start | bytes 52
  30.2 14.9 %collective-permute-start = (bf16[2,256,512]{2,1,0:T(8,128)(2,1)}, bf16[2,256,512]{2,1,0:T(8,128)(2,1)S(1)}, u32[]{:S(2)}, u32[]{:S(2)}) collective-permute-start(bf16[2,256,512]{2,1,0:T(8,128)(2,1)} %pad_maximum_fusion), channel_id=1, source_target_pairs={{0,1},{1,2},{2,3},{3,0},{4,5},{5,6},{6,7},{7,4},{8,9},{9,10},{10,1... | collective-permute-start | bytes 1572872 | tf_op jit(solution)/shard_map/ppermute | solution.py:153
  45.2 14.0 %collective-permute-start.1 = (bf16[2,256,512]{2,1,0:T(8,128)(2,1)S(1)}, bf16[2,256,512]{2,1,0:T(8,128)(2,1)}, u32[]{:S(2)}, u32[]{:S(2)}) collective-permute-start(bf16[2,256,512]{2,1,0:T(8,128)(2,1)S(1)} %collective-permute-done), channel_id=1, source_target_pairs={{0,1},{1,2},{2,3},{3,0},{4,5},{5,6},{6,7},{7,4},{8,9},{9,10},{10,1... | collective-permute-start | bytes 1572872 | tf_op jit(solution)/shard_map/ppermute | solution.py:153
  45.8 13.4 %copy-start.34 = (s32[256]{0:T(256)}, s32[256]{0:T(256)S(1)}, u32[]{:S(2)}) copy-start(s32[256]{0:T(256)S(1)} %get-tuple-element.23) | copy-start | bytes 3076
  59.1 13.3 %collective-permute-start.2 = (bf16[2,256,512]{2,1,0:T(8,128)(2,1)}, bf16[2,256,512]{2,1,0:T(8,128)(2,1)}, u32[]{:S(2)}, u32[]{:S(2)}) collective-permute-start(bf16[2,256,512]{2,1,0:T(8,128)(2,1)} %collective-permute-done.1), channel_id=1, source_target_pairs={{0,1},{1,2},{2,3},{3,0},{4,5},{5,6},{6,7},{7,4},{8,9},{9,10},{10,1... | collective-permute-start | bytes 1572872 | tf_op jit(solution)/shard_map/ppermute | solution.py:153
  88.0 8.8 %copy-start.5 = (f32[1,1024]{1,0:T(1,128)S(1)}, f32[1,1024]{1,0:T(1,128)}, u32[]{:S(2)}) copy-start(f32[1,1024]{1,0:T(1,128)} %get-tuple-element.64) | copy-start | bytes 12292
  88.0 8.8 %copy-start.6 = (f32[1,1024]{1,0:T(1,128)S(1)}, f32[1,1024]{1,0:T(1,128)}, u32[]{:S(2)}) copy-start(f32[1,1024]{1,0:T(1,128)} %get-tuple-element.65) | copy-start | bytes 12292
  88.0 8.8 %copy-start.7 = (f32[1,1024]{1,0:T(1,128)S(1)}, f32[1,1024]{1,0:T(1,128)}, u32[]{:S(2)}) copy-start(f32[1,1024]{1,0:T(1,128)} %get-tuple-element.66) | copy-start | bytes 12292
  88.0 8.8 %copy-start.8 = (f32[1,1024]{1,0:T(1,128)S(1)}, f32[1,1024]{1,0:T(1,128)}, u32[]{:S(2)}) copy-start(f32[1,1024]{1,0:T(1,128)} %get-tuple-element.67) | copy-start | bytes 12292
  88.0 8.8 %copy-start.9 = (f32[1,1024]{1,0:T(1,128)S(1)}, f32[1,1024]{1,0:T(1,128)}, u32[]{:S(2)}) copy-start(f32[1,1024]{1,0:T(1,128)} %get-tuple-element.68) | copy-start | bytes 12292
  88.0 8.8 %copy-start.10 = (f32[1,1024]{1,0:T(1,128)S(1)}, f32[1,1024]{1,0:T(1,128)}, u32[]{:S(2)}) copy-start(f32[1,1024]{1,0:T(1,128)} %get-tuple-element.69) | copy-start | bytes 12292
  88.0 8.8 %copy-start.11 = (f32[1,1024]{1,0:T(1,128)S(1)}, f32[1,1024]{1,0:T(1,128)}, u32[]{:S(2)}) copy-start(f32[1,1024]{1,0:T(1,128)} %get-tuple-element.70) | copy-start | bytes 12292
  88.0 8.8 %copy-start.12 = (f32[1,1024]{1,0:T(1,128)S(1)}, f32[1,1024]{1,0:T(1,128)}, u32[]{:S(2)}) copy-start(f32[1,1024]{1,0:T(1,128)} %get-tuple-element.71) | copy-start | bytes 12292
  88.0 8.8 %copy-start.13 = (f32[1,1024]{1,0:T(1,128)S(1)}, f32[1,1024]{1,0:T(1,128)}, u32[]{:S(2)}) copy-start(f32[1,1024]{1,0:T(1,128)} %get-tuple-element.72) | copy-start | bytes 12292
  88.0 8.8 %copy-start.14 = (f32[1,1024]{1,0:T(1,128)S(1)}, f32[1,1024]{1,0:T(1,128)}, u32[]{:S(2)}) copy-start(f32[1,1024]{1,0:T(1,128)} %get-tuple-element.73) | copy-start | bytes 12292
  88.1 8.8 %copy-start.15 = (f32[1,1024]{1,0:T(1,128)S(1)}, f32[1,1024]{1,0:T(1,128)}, u32[]{:S(2)}) copy-start(f32[1,1024]{1,0:T(1,128)} %get-tuple-element.43) | copy-start | bytes 12292
  88.1 8.8 %copy-start.16 = (f32[1,1024]{1,0:T(1,128)S(1)}, f32[1,1024]{1,0:T(1,128)}, u32[]{:S(2)}) copy-start(f32[1,1024]{1,0:T(1,128)} %get-tuple-element.44) | copy-start | bytes 12292
  88.1 8.8 %copy-start.17 = (f32[1,1024]{1,0:T(1,128)S(1)}, f32[1,1024]{1,0:T(1,128)}, u32[]{:S(2)}) copy-start(f32[1,1024]{1,0:T(1,128)} %get-tuple-element.45) | copy-start | bytes 12292
  88.1 8.8 %copy-start.18 = (f32[1,1024]{1,0:T(1,128)S(1)}, f32[1,1024]{1,0:T(1,128)}, u32[]{:S(2)}) copy-start(f32[1,1024]{1,0:T(1,128)} %get-tuple-element.46) | copy-start | bytes 12292
  88.1 8.8 %copy-start.19 = (f32[1,1024]{1,0:T(1,128)S(1)}, f32[1,1024]{1,0:T(1,128)}, u32[]{:S(2)}) copy-start(f32[1,1024]{1,0:T(1,128)} %get-tuple-element.47) | copy-start | bytes 12292
  88.1 8.8 %copy-start.20 = (f32[1,1024]{1,0:T(1,128)S(1)}, f32[1,1024]{1,0:T(1,128)}, u32[]{:S(2)}) copy-start(f32[1,1024]{1,0:T(1,128)} %get-tuple-element.48) | copy-start | bytes 12292
  88.1 8.8 %copy-start.21 = (f32[1,1024]{1,0:T(1,128)S(1)}, f32[1,1024]{1,0:T(1,128)}, u32[]{:S(2)}) copy-start(f32[1,1024]{1,0:T(1,128)} %get-tuple-element.49) | copy-start | bytes 12292
  88.1 8.8 %copy-start.22 = (f32[1,1024]{1,0:T(1,128)S(1)}, f32[1,1024]{1,0:T(1,128)}, u32[]{:S(2)}) copy-start(f32[1,1024]{1,0:T(1,128)} %get-tuple-element.50) | copy-start | bytes 12292
  88.1 8.8 %copy-start.23 = (f32[1,1024]{1,0:T(1,128)S(1)}, f32[1,1024]{1,0:T(1,128)}, u32[]{:S(2)}) copy-start(f32[1,1024]{1,0:T(1,128)} %get-tuple-element.51) | copy-start | bytes 12292
  88.2 8.8 %copy-start.24 = (f32[1,1024]{1,0:T(1,128)S(1)}, f32[1,1024]{1,0:T(1,128)}, u32[]{:S(2)}) copy-start(f32[1,1024]{1,0:T(1,128)} %get-tuple-element.52) | copy-start | bytes 12292
  88.2 8.8 %copy-start.25 = (f32[1,1024]{1,0:T(1,128)S(1)}, f32[1,1024]{1,0:T(1,128)}, u32[]{:S(2)}) copy-start(f32[1,1024]{1,0:T(1,128)} %get-tuple-element.53) | copy-start | bytes 12292
  88.2 8.8 %copy-start.26 = (f32[1,1024]{1,0:T(1,128)S(1)}, f32[1,1024]{1,0:T(1,128)}, u32[]{:S(2)}) copy-start(f32[1,1024]{1,0:T(1,128)} %get-tuple-element.54) | copy-start | bytes 12292
  89.5 2.9 %collective-permute-start.3 = (bf16[15,1024]{1,0:T(8,128)(2,1)S(1)}, bf16[15,1024]{1,0:T(8,128)(2,1)S(1)}, u32[]{:S(2)}, u32[]{:S(2)}) collective-permute-start(bf16[15,1024]{1,0:T(8,128)(2,1)S(1)} %get-tuple-element.41), channel_id=1, source_target_pairs={{0,1},{1,2},{2,3},{4,5},{5,6},{6,7},{8,9},{9,10},{10,11},{12,13},{... | collective-permute-start | bytes 92168 | tf_op jit(solution)/shard_map/ppermute | solution.py:19
  90.8 5.8 %collective-permute-start.4 = (bf16[15,1024]{1,0:T(8,128)(2,1)S(1)}, bf16[15,1024]{1,0:T(8,128)(2,1)S(1)}, u32[]{:S(2)}, u32[]{:S(2)}) collective-permute-start(bf16[15,1024]{1,0:T(8,128)(2,1)S(1)} %get-tuple-element.42), channel_id=1, source_target_pairs={{1,0},{2,1},{3,2},{5,4},{6,5},{7,6},{9,8},{10,9},{11,10},{13,12},{... | collective-permute-start | bytes 92168 | tf_op jit(solution)/shard_map/ppermute | solution.py:22
  (19 other events, 149.5 us)
